TPU v7x, 32 devices: a whole 2x2x4 slice. The times are simulated.
32 devices in a mesh: grp: 2 (over y), slab: 16 (over z, x, core).
Axes of the slice: x: 2, y: 2, z: 4, core: 2. Of those that a mesh axis runs over, the one named last changes fastest.
Arguments:
- velocity: float32 [16, 128, 512], P('grp', 'slab'), may hold values from -6 to 6
- rate: float32 [16, 128, 512], P('grp', 'slab'), may hold values from 0.02 to 0.16
- forcing: float32 [16, 128, 512], P('grp', 'slab'), may hold values from -3 to 3
- anchor_line: int32 [512], P(('grp', 'slab')), may hold values from 0 to 63
- anchor_z: int32 [512], P(('grp', 'slab')), may hold values from 0 to 384
- assign: int32 [512, 1], P(('grp', 'slab')), may hold values from 0 to 15; in each aligned block of 16 rows (0 to 15, 16 to 31, ...) at most 2 rows name the same one
- spectral: float32 [2048, 64], replicated, may hold values from -0.75 to 0.75
- dense: float32 [68, 64], replicated, may hold values from -4 to 4
- momentum: float32 [2048, 64], P(('grp', 'slab')), may hold values from -0.3125 to 0.3125
Outputs:
- field_out: float32 [16, 128, 512], P('grp', 'slab')
- trainer_loss: float32 [2, 16], P('grp', 'slab')
- spectral_new: float32 [2048, 64], replicated
- dense_new: float32 [68, 64], replicated
- momentum_new: float32 [2048, 64], P(('grp', 'slab'))
Inputs may be any that keep to these rules, and one draw needn't show every extreme that they name: `assign`: within the 16 lines of one device no trainer is named more than 2 times, and in some device's lines one trainer is named exactly 2 times.
All inputs are finite; a program needn't handle non-finite values.
Results may differ from a plain program's by a relative error of at most 0.0001.
Values sent between devices are 32-bit elements; how exact they have to be, the bound alone decides.
No kernel may reach another device: no remote copies, remote signals or barrier semaphores. Data moves between devices by JAX's collectives and lax.ppermute only.
A program may use at most 64 MiB of HBM per device.

v0:
```python
import jax
import jax.numpy as jnp
from jax import lax
from jax.sharding import PartitionSpec as P

STEPS = 2
SUB = 128
MODES = 16
decay_rate = 0.9
learn_rate = 0.5
dense_rate = 3.0


def extended(cells, sides, width):
    for axis, dim in sides:
        count = lax.axis_size(axis)
        ends = count - 1
        head = lax.slice_in_dim(cells, 0, width, axis=dim)
        tail = lax.slice_in_dim(cells, cells.shape[dim] - width, cells.shape[dim], axis=dim)
        cells = jnp.concatenate(
            [
                lax.ppermute(tail, axis, [(i, (i + 1) % count) for i in range(ends)]),
                cells,
                lax.ppermute(head, axis, [((i + 1) % count, i) for i in range(ends)]),
            ],
            axis=dim,
        )
    return cells


def tables():
    counts = jnp.arange(SUB, dtype=jnp.int32)
    waves = jnp.arange(MODES, dtype=jnp.int32)
    phase = counts[:, None] * waves[None, :] % SUB
    angle = phase.astype(jnp.float32) * (2.0 * jnp.pi / SUB)
    weight_k = jnp.where(waves == 0, 1.0, 2.0).astype(jnp.float32) / SUB
    return (jnp.cos(angle), jnp.sin(angle), weight_k)


def line_errors(spectral, dense, inputs, targets, valid):
    highest = lax.Precision.HIGHEST
    width = dense.shape[1]
    mixing = dense[:width]
    lift_gain, lift_bias, layer_bias, projection = (
        dense[width],
        dense[width + 1],
        dense[width + 2],
        dense[width + 3],
    )
    cosine, sine, weight_k = tables()
    hidden = inputs[:, None, :] * lift_gain[None, :, None] + lift_bias[None, :, None]
    real_in = jnp.einsum("bws,sk->bwk", hidden, cosine, precision=highest)
    imag_in = -jnp.einsum("bws,sk->bwk", hidden, sine, precision=highest)
    blocks = spectral.reshape(2, MODES, width, width)
    w_real, w_imag = (blocks[0], blocks[1])
    real_out = jnp.einsum("bwk,kwv->bvk", real_in, w_real, precision=highest) - jnp.einsum(
        "bwk,kwv->bvk", imag_in, w_imag, precision=highest
    )
    imag_out = jnp.einsum("bwk,kwv->bvk", real_in, w_imag, precision=highest) + jnp.einsum(
        "bwk,kwv->bvk", imag_in, w_real, precision=highest
    )
    spatial = jnp.einsum(
        "bvk,sk->bvs", real_out * weight_k, cosine, precision=highest
    ) - jnp.einsum("bvk,sk->bvs", imag_out * weight_k, sine, precision=highest)
    before = (
        spatial
        + jnp.einsum("bws,wv->bvs", hidden, mixing, precision=highest)
        + layer_bias[None, :, None]
    )
    after = jax.nn.gelu(before)
    output = jnp.einsum("bvs,v->bs", after, projection, precision=highest)
    return jnp.sum((output - targets) ** 2, axis=1) * valid


def gradients_of(spectral, dense, inputs, targets, valid, scale):

    def loss_fn(spec, dens):
        errors = line_errors(spec, dens, inputs, targets, valid)
        return (jnp.sum(errors) * scale, errors)

    value, pullback, errors = jax.vjp(loss_fn, spectral, dense, has_aux=True)
    grad_spec, grad_dense = pullback(jnp.ones((), jnp.float32))
    return (grad_spec, grad_dense, errors)


def local(velocity, rate, forcing, anchor_line, anchor_z, assign, spectral, dense, momentum):
    field_now = velocity
    previous = velocity
    change = velocity
    for number in range(STEPS):
        previous = field_now
        padded = extended(field_now, (("grp", 0), ("slab", 1)), 1)
        beside = padded[2:, 1:-1] + padded[:-2, 1:-1] + padded[1:-1, 2:] + padded[1:-1, :-2]
        beside = beside + jnp.roll(field_now, 1, 2) + jnp.roll(field_now, -1, 2)
        change = rate * (beside - 6.0 * field_now) + forcing
        field_now = field_now + change
    cells_x, cells_y, cells_z = velocity.shape
    line_count = anchor_line.shape[0]
    windows = jax.vmap(lambda row, start: lax.dynamic_slice_in_dim(row, start, SUB))
    inputs = windows(
        jnp.take(previous.reshape(cells_x * cells_y, cells_z), anchor_line, axis=0), anchor_z
    )
    targets = windows(
        jnp.take(change.reshape(cells_x * cells_y, cells_z), anchor_line, axis=0), anchor_z
    )
    n_slab = lax.axis_size("slab")
    devices = lax.axis_size("grp") * n_slab
    scale = 1.0 / (devices * line_count * SUB)
    dest = assign[:, 0]
    onehot = (dest[:, None] == jnp.arange(n_slab, dtype=jnp.int32)[None, :]).astype(jnp.int32)
    grad_spec, grad_dense, errors = gradients_of(
        spectral, dense, inputs, targets, jnp.ones((line_count,), jnp.float32), scale
    )
    partial_loss = jnp.dot(errors, onehot.astype(jnp.float32), precision=lax.Precision.HIGHEST) / (
        line_count * SUB
    )
    trainer_loss = lax.psum_scatter(partial_loss, "slab", scatter_dimension=0, tiled=True).reshape(
        1, 1
    )
    grad_rows = lax.psum_scatter(grad_spec, ("grp", "slab"), scatter_dimension=0, tiled=True)
    grad_dense = lax.psum(grad_dense, ("grp", "slab"))
    piece_rows = grad_rows.shape[0]
    position = lax.axis_index(("grp", "slab"))
    own_rows = lax.dynamic_slice_in_dim(spectral, position * piece_rows, piece_rows, 0)
    momentum_new = decay_rate * momentum + grad_rows
    updated_rows = own_rows - learn_rate * momentum_new
    spectral_new = lax.all_gather(updated_rows, ("grp", "slab"), axis=0, tiled=True)
    dense_new = dense - dense_rate * grad_dense
    return (field_now, trainer_loss, spectral_new, dense_new, momentum_new)


def solution(mesh):
    placed = (
        P("grp", "slab", None),
        P("grp", "slab", None),
        P("grp", "slab", None),
        P(("grp", "slab")),
        P(("grp", "slab")),
        P(("grp", "slab"), None),
        P(),
        P(),
        P(("grp", "slab"), None),
    )
    return jax.shard_map(
        local,
        mesh=mesh,
        in_specs=placed,
        out_specs=(P("grp", "slab", None), P("grp", "slab"), P(), P(), P(("grp", "slab"), None)),
        check_vma=False,
    )
```

profile of v0, /device:TPU:0, one launch (start us, length us, event | category | flops | bytes accessed | tf_op | source)
XLA Modules:
  0.0 314.7 jit_solution(17592519083051629129)
XLA Ops:
  9.3 4.9 %collective-permute-start.1 = (f32[1,8,512]{2,1,0:T(8,128)S(1)}, f32[1,8,512]{2,1,0:T(8,128)S(1)}, u32[]{:S(2)}, u32[]{:S(2)}) collective-permute-start(f32[1,8,512]{2,1,0:T(8,128)S(1)} %get-tuple-element.86), channel_id=1, source_target_pairs={{0,16},{1,17},{2,18},{3,19},{4,20},{5,21},{6,22},{7,23},{8,24},{9,... | collective-permute-start | bytes 49160 | tf_op jit(solution)/shard_map/ppermute | solution.py:22
  19.0 3.0 collective-permute-start.3
  24.0 2.3 collective-permute-start.5
  27.6 4.2 %collective-permute-done.4 = f32[1,8,512]{2,1,0:T(8,128)S(1)} collective-permute-done((f32[1,8,512]{2,1,0:T(8,128)S(1)}, f32[1,8,512]{2,1,0:T(8,128)S(1)}, u32[]{:S(2)}, u32[]{:S(2)}) %collective-permute-start.4) | collective-permute-done | bytes 16416 | tf_op jit(solution)/shard_map/ppermute | solution.py:24
  33.2 3.3 %collective-permute-start.7 = (f32[10,1,512]{2,1,0:T(1,128)S(1)}, f32[10,1,512]{2,1,0:T(1,128)S(1)}, u32[]{:S(2)}, u32[]{:S(2)}) collective-permute-start(f32[10,1,512]{2,1,0:T(1,128)S(1)} %get-tuple-element.72), channel_id=1, source_target_pairs={{0,1},{1,2},{2,3},{3,4},{4,5},{5,6},{6,7},{7,8},{8,9},{9,10},{10,1... | collective-permute-start | bytes 61448 | tf_op jit(solution)/shard_map/ppermute | solution.py:22
  38.8 32.3 %while.2 = (s32[]{:T(128)}, f32[16,512]{1,0:T(8,128)S(1)}, s32[16,2]{0,1:T(2,128)S(1)}, f32[16,128]{1,0:T(8,128)S(1)}, s32[]{:T(128)}, /*index=5*/s32[]{:T(128)}) while((s32[]{:T(128)}, f32[16,512]{1,0:T(8,128)S(1)}, s32[16,2]{0,1:T(2,128)S(1)}, f32[16,128]{1,0:T(8,128)S(1)}, s32[]{:T(128)}, /*index=5*/s32[]{:T(128)}) %tuple.61), condition=%wide.while_cond, body=%wide.while_body.sunk | while | flops 2 | bytes 2169 | solution.py:99
  39.4 1.3 dynamic-slice.15
  41.5 1.3 dynamic-slice.15
  43.5 1.3 dynamic-slice.15
  45.5 1.3 dynamic-slice.15
  47.5 1.3 dynamic-slice.15
  49.5 1.3 dynamic-slice.15
  51.5 1.3 dynamic-slice.15
  53.6 1.3 dynamic-slice.15
  55.6 1.3 dynamic-slice.15
  57.6 1.3 dynamic-slice.15
  59.6 1.3 dynamic-slice.15
  61.6 1.3 dynamic-slice.15
  63.7 1.3 dynamic-slice.15
  65.7 1.3 dynamic-slice.15
  67.7 1.3 dynamic-slice.15
  69.7 1.3 dynamic-slice.15
  71.1 1.4 convolution_negate_fusion
  72.5 1.4 fusion.38
  74.7 32.1 %while.3 = (s32[]{:T(128)}, f32[16,512]{1,0:T(8,128)S(1)}, s32[16,2]{0,1:T(2,128)S(1)}, f32[16,128]{1,0:T(8,128)S(1)}, s32[]{:T(128)}, /*index=5*/s32[]{:T(128)}) while((s32[]{:T(128)}, f32[16,512]{1,0:T(8,128)S(1)}, s32[16,2]{0,1:T(2,128)S(1)}, f32[16,128]{1,0:T(8,128)S(1)}, s32[]{:T(128)}, /*index=5*/s32[]{:T(128)}) %tuple.69), condition=%wide.while_cond.1, body=%wide.while_body.1.sunk | while | flops 2 | bytes 2169 | solution.py:99
  75.3 1.4 dynamic-slice.17
  77.3 1.4 dynamic-slice.17
  79.3 1.4 dynamic-slice.17
  81.2 1.4 dynamic-slice.17
  83.2 1.4 dynamic-slice.17
  85.2 1.4 dynamic-slice.17
  87.2 1.4 dynamic-slice.17
  89.2 1.4 dynamic-slice.17
  91.2 1.4 dynamic-slice.17
  93.2 1.4 dynamic-slice.17
  95.2 1.4 dynamic-slice.17
  97.2 1.4 dynamic-slice.17
  99.2 1.4 dynamic-slice.17
  101.2 1.4 dynamic-slice.17
  103.2 1.4 dynamic-slice.17
  105.2 1.4 dynamic-slice.17
  112.4 1.3 fusion.6
  113.8 1.4 fusion.186
  126.2 35.7 %all-reduce.7 = f32[16]{0:T(128)S(1)} all-reduce(f32[16]{0:T(128)S(1)} %fusion.11), channel_id=2, replica_groups=mesh['grp'=2,'slab'=16] {'slab'}, use_global_device_ids=true, to_apply=%region_1.3.clone | all-reduce | flops 16 | bytes 128
  167.0 37.0 %psum.7 = f32[68,64]{0,1:T(8,128)S(1)} all-reduce(f32[68,64]{0,1:T(8,128)S(1)} %pad_add_fusion.1), channel_id=1, replica_groups=mesh['grp'=2,'slab'=16] {'grp','slab'}, use_global_device_ids=true, to_apply=%region_6.8 | all-reduce | flops 4352 | bytes 34816 | tf_op jit(solution)/shard_map/psum | solution.py:121
  204.6 61.4 %reduce-scatter.2.cloned.1.call-done = f32[64,64]{1,0:T(8,128)} async-done(((f32[2048,64]{1,0:T(8,128)}), f32[64,64]{1,0:T(8,128)}) %reduce-scatter.2.cloned.1.call-update) | async-done | bytes 16400 | tf_op jit(solution)/shard_map/reduce_scatter | solution.py:120
  266.1 1.4 multiply_subtract_fusion.1
  267.5 39.3 %all_gather.3 = f32[2048,64]{1,0:T(8,128)S(1)} all-gather(f32[64,64]{1,0:T(8,128)S(1)} %get-tuple-element.61), channel_id=1, replica_groups=mesh['grp'=2,'slab'=16] {'grp','slab'}, dimensions={0}, use_global_device_ids=true | all-gather | bytes 540672 | tf_op jit(solution)/shard_map/all_gather | solution.py:127
  (192 shorter events, 58.4 us)
Async XLA Ops:
  7.2 9.2 %copy-start = (f32[8,8,512]{2,1,0:T(8,128)S(1)}, f32[8,8,512]{2,1,0:T(8,128)}, u32[]{:S(2)}) copy-start(f32[8,8,512]{2,1,0:T(8,128)} %param.11) | copy-start | bytes 393220
  7.2 10.2 %copy-start.2 = (f32[2048,64]{0,1:T(8,128)S(1)}, f32[2048,64]{0,1:T(8,128)}, u32[]{:S(2)}) copy-start(f32[2048,64]{0,1:T(8,128)} %param.17) | copy-start | bytes 1572868
  7.2 258.9 %reduce-scatter.2.cloned.1.call-start = ((), (), s32[]{:S(2)}) async-start(), calls=%async_computation.1 | async-start | bytes 1081344 | tf_op jit(solution)/shard_map/reduce_scatter | solution.py:120
  8.0 9.6 %collective-permute-start = (f32[1,8,512]{2,1,0:T(8,128)S(1)}, f32[1,8,512]{2,1,0:T(8,128)S(1)}, u32[]{:S(2)}, u32[]{:S(2)}) collective-permute-start(f32[1,8,512]{2,1,0:T(8,128)S(1)} %get-tuple-element.85), channel_id=1, source_target_pairs={{16,0},{17,1},{18,2},{19,3},{20,4},{21,5},{22,6},{23,7},{24,8},{25... | collective-permute-start | bytes 49160 | tf_op jit(solution)/shard_map/ppermute | solution.py:24
  9.3 8.3 %collective-permute-start.1 = (f32[1,8,512]{2,1,0:T(8,128)S(1)}, f32[1,8,512]{2,1,0:T(8,128)S(1)}, u32[]{:S(2)}, u32[]{:S(2)}) collective-permute-start(f32[1,8,512]{2,1,0:T(8,128)S(1)} %get-tuple-element.86), channel_id=1, source_target_pairs={{0,16},{1,17},{2,18},{3,19},{4,20},{5,21},{6,22},{7,23},{8,24},{9,... | collective-permute-start | bytes 49160 | tf_op jit(solution)/shard_map/ppermute | solution.py:22
  16.4 0.8 copy-start.1
  16.5 0.7 copy-start.6
  17.7 6.1 %collective-permute-start.2 = (f32[10,1,512]{2,1,0:T(1,128)S(1)}, f32[10,1,512]{2,1,0:T(1,128)S(1)}, u32[]{:S(2)}, u32[]{:S(2)}) collective-permute-start(f32[10,1,512]{2,1,0:T(1,128)S(1)} %get-tuple-element.73), channel_id=1, source_target_pairs={{1,0},{2,1},{3,2},{4,3},{5,4},{6,5},{7,6},{8,7},{9,8},{10,9},{11,1... | collective-permute-start | bytes 61448 | tf_op jit(solution)/shard_map/ppermute | solution.py:24
  19.0 4.8 %collective-permute-start.3 = (f32[10,1,512]{2,1,0:T(1,128)S(1)}, f32[10,1,512]{2,1,0:T(1,128)S(1)}, u32[]{:S(2)}, u32[]{:S(2)}) collective-permute-start(f32[10,1,512]{2,1,0:T(1,128)S(1)} %get-tuple-element.74), channel_id=1, source_target_pairs={{0,1},{1,2},{2,3},{3,4},{4,5},{5,6},{6,7},{7,8},{8,9},{9,10},{10,1... | collective-permute-start | bytes 61448 | tf_op jit(solution)/shard_map/ppermute | solution.py:22
  22.3 1.5 copy-start.3
  22.3 1.5 copy-start.4
  22.5 0.7 copy-start.8
  24.0 3.7 %collective-permute-start.5 = (f32[1,8,512]{2,1,0:T(8,128)S(1)}, f32[1,8,512]{2,1,0:T(8,128)S(1)}, u32[]{:S(2)}, u32[]{:S(2)}) collective-permute-start(f32[1,8,512]{2,1,0:T(8,128)S(1)} %get-tuple-element.75), channel_id=1, source_target_pairs={{0,16},{1,17},{2,18},{3,19},{4,20},{5,21},{6,22},{7,23},{8,24},{9,... | collective-permute-start | bytes 49160 | tf_op jit(solution)/shard_map/ppermute | solution.py:22
  26.2 5.6 %collective-permute-start.4 = (f32[1,8,512]{2,1,0:T(8,128)S(1)}, f32[1,8,512]{2,1,0:T(8,128)S(1)}, u32[]{:S(2)}, u32[]{:S(2)}) collective-permute-start(f32[1,8,512]{2,1,0:T(8,128)S(1)} %get-tuple-element.76), channel_id=1, source_target_pairs={{16,0},{17,1},{18,2},{19,3},{20,4},{21,5},{22,6},{23,7},{24,8},{25... | collective-permute-start | bytes 49160 | tf_op jit(solution)/shard_map/ppermute | solution.py:24
  31.9 5.3 %collective-permute-start.6 = (f32[10,1,512]{2,1,0:T(1,128)S(1)}, f32[10,1,512]{2,1,0:T(1,128)S(1)}, u32[]{:S(2)}, u32[]{:S(2)}) collective-permute-start(f32[10,1,512]{2,1,0:T(1,128)S(1)} %get-tuple-element.71), channel_id=1, source_target_pairs={{1,0},{2,1},{3,2},{4,3},{5,4},{6,5},{7,6},{8,7},{9,8},{10,9},{11,1... | collective-permute-start | bytes 61448 | tf_op jit(solution)/shard_map/ppermute | solution.py:24
  33.2 4.2 %collective-permute-start.7 = (f32[10,1,512]{2,1,0:T(1,128)S(1)}, f32[10,1,512]{2,1,0:T(1,128)S(1)}, u32[]{:S(2)}, u32[]{:S(2)}) collective-permute-start(f32[10,1,512]{2,1,0:T(1,128)S(1)} %get-tuple-element.72), channel_id=1, source_target_pairs={{0,1},{1,2},{2,3},{3,4},{4,5},{5,6},{6,7},{7,8},{8,9},{9,10},{10,1... | collective-permute-start | bytes 61448 | tf_op jit(solution)/shard_map/ppermute | solution.py:22
  124.5 0.7 copy-start.7
  204.0 62.1 %copy-start.5 = (f32[64,64]{1,0:T(8,128)S(1)}, f32[64,64]{1,0:T(8,128)}, u32[]{:S(2)}) copy-start(f32[64,64]{1,0:T(8,128)} %param.19) | copy-start | bytes 49156
Sparse Core Ops, SparseCore 0:
  124.6 141.4 reduce-scatter.1
where the time goes:
time: 316 us; the launch traced here: 315 us
  blocking collectives  112 us (35%)
  local copies, waits for them, and re-layouts  73.2 us (23%)
  waiting for transfers between devices  65.9 us (21%)
  matrix products  23.5 us (7%)
  starting transfers between devices  18.7 us (6%)
  between operations  14.5 us (5%)
  other arithmetic  6.66 us (2%)
    gather x128, local copies, waits for them, and re-layouts  64.1 us
    reduce_scatter x1, waiting for transfers between devices, local(): lax.psum_scatter(grad_spec, ('grp', 'slab'), scatter_dimension=0, tiled=T...  61.4 us
    all_gather x1, blocking collectives, local(): lax.all_gather(updated_rows, ('grp', 'slab'), axis=0, tiled=True)  39.3 us
    psum x1, blocking collectives, local(): grad_dense = lax.psum(grad_dense, ('grp', 'slab'))  37 us
    unnamed x1, blocking collectives  35.7 us
    ppermute x4, starting transfers between devices, extended(): lax.ppermute(tail, axis, [(i, (i + 1) % count) for i in range(ends)])  13.5 us
  transfers between devices with their start and end apart: 9, of which 3 were waited for; matrix products, arithmetic and copies ran while one was open for 4% of the time, Pallas kernels for 0%

commit v1 on v0

--- a/solution.py
+++ b/solution.py
@@ -118,7 +118,7 @@
         1, 1
     )
     grad_rows = lax.psum_scatter(grad_spec, ("grp", "slab"), scatter_dimension=0, tiled=True)
-    grad_dense = lax.psum(grad_dense, ("grp", "slab"))
+    grad_dense = jnp.sum(lax.all_gather(grad_dense, ("grp", "slab")), axis=0)
     piece_rows = grad_rows.shape[0]
     position = lax.axis_index(("grp", "slab"))
     own_rows = lax.dynamic_slice_in_dim(spectral, position * piece_rows, piece_rows, 0)

time: 316 us -> 349 us (1.10)
  waiting for transfers between devices: 65.9 us -> 91.9 us
  matrix products: 23.5 us -> 27.7 us
    all_gather x0 -> x1, blocking collectives: none -> 39.7 us  [local(): grad_dense = jnp.sum(lax.all_gather(grad_dense, ('grp', 'slab')), axis=0)]
    psum x1 -> x0, blocking collectives: 37 us -> none  [local(): grad_dense = lax.psum(grad_dense, ('grp', 'slab'))]
    reduce_scatter x1, waiting for transfers between devices: 61.4 us -> 87.5 us  [local(): lax.psum_scatter(grad_spec, ('grp', 'slab'), scatter_dimension=0, tiled=T...]
  transfers between devices with their start and end apart: 9 -> 9, of which waited for: 3 -> 3; matrix products, arithmetic and copies ran while one was open for 4% -> 3% of each run, Pallas kernels for 0% -> 0%
where the time goes in v1:
time: 349 us; the launch traced here: 348 us
  blocking collectives  115 us (33%)
  waiting for transfers between devices  91.9 us (26%)
  local copies, waits for them, and re-layouts  73.1 us (21%)
  matrix products  27.7 us (8%)
  starting transfers between devices  18.7 us (5%)
  between operations  14.5 us (4%)
  other arithmetic  6.79 us (2%)
    reduce_scatter x1, waiting for transfers between devices, local(): lax.psum_scatter(grad_spec, ('grp', 'slab'), scatter_dimension=0, tiled=T...  87.5 us
    gather x128, local copies, waits for them, and re-layouts  63.9 us
    all_gather x1, blocking collectives, local(): grad_dense = jnp.sum(lax.all_gather(grad_dense, ('grp', 'slab')), axis=0)  39.7 us
    all_gather x1, blocking collectives, local(): lax.all_gather(updated_rows, ('grp', 'slab'), axis=0, tiled=True)  39.3 us
    unnamed x1, blocking collectives  35.6 us
    ppermute x4, starting transfers between devices, extended(): lax.ppermute(tail, axis, [(i, (i + 1) % count) for i in range(ends)])  13.5 us
  transfers between devices with their start and end apart: 9, of which 3 were waited for; matrix products, arithmetic and copies ran while one was open for 3% of the time, Pallas kernels for 0%

profile of v1, /device:TPU:0, one launch (start us, length us, event | category | flops | bytes accessed | tf_op | source)
XLA Modules:
  0.0 347.6 jit_solution(13756954468196533733)
XLA Ops:
  9.3 4.9 %collective-permute-start.1 = (f32[1,8,512]{2,1,0:T(8,128)S(1)}, f32[1,8,512]{2,1,0:T(8,128)S(1)}, u32[]{:S(2)}, u32[]{:S(2)}) collective-permute-start(f32[1,8,512]{2,1,0:T(8,128)S(1)} %get-tuple-element.86), channel_id=1, source_target_pairs={{0,16},{1,17},{2,18},{3,19},{4,20},{5,21},{6,22},{7,23},{8,24},{9,... | collective-permute-start | bytes 49160 | tf_op jit(solution)/shard_map/ppermute | solution.py:22
  19.0 3.0 collective-permute-start.3
  24.0 2.3 collective-permute-start.5
  27.6 4.2 %collective-permute-done.4 = f32[1,8,512]{2,1,0:T(8,128)S(1)} collective-permute-done((f32[1,8,512]{2,1,0:T(8,128)S(1)}, f32[1,8,512]{2,1,0:T(8,128)S(1)}, u32[]{:S(2)}, u32[]{:S(2)}) %collective-permute-start.4) | collective-permute-done | bytes 16416 | tf_op jit(solution)/shard_map/ppermute | solution.py:24
  33.2 3.3 collective-permute-start.7
  38.8 32.1 %while.2 = (s32[]{:T(128)}, f32[16,512]{1,0:T(8,128)S(1)}, s32[16,2]{0,1:T(2,128)S(1)}, f32[16,128]{1,0:T(8,128)S(1)}, s32[]{:T(128)}, /*index=5*/s32[]{:T(128)}) while((s32[]{:T(128)}, f32[16,512]{1,0:T(8,128)S(1)}, s32[16,2]{0,1:T(2,128)S(1)}, f32[16,128]{1,0:T(8,128)S(1)}, s32[]{:T(128)}, /*index=5*/s32[]{:T(128)}) %tuple.61), condition=%wide.while_cond, body=%wide.while_body.sunk | while | flops 2 | bytes 2169 | solution.py:99
  39.4 1.4 dynamic-slice.15
  41.4 1.4 dynamic-slice.15
  43.4 1.4 dynamic-slice.15
  45.4 1.4 dynamic-slice.15
  47.4 1.4 dynamic-slice.15
  49.4 1.4 dynamic-slice.15
  51.4 1.4 dynamic-slice.15
  53.4 1.4 dynamic-slice.15
  55.5 1.4 dynamic-slice.15
  57.5 1.4 dynamic-slice.15
  59.5 1.4 dynamic-slice.15
  61.5 1.4 dynamic-slice.15
  63.5 1.4 dynamic-slice.15
  70.9 1.4 convolution_negate_fusion
  72.3 1.4 fusion.38
  74.4 32.1 %while.3 = (s32[]{:T(128)}, f32[16,512]{1,0:T(8,128)S(1)}, s32[16,2]{0,1:T(2,128)S(1)}, f32[16,128]{1,0:T(8,128)S(1)}, s32[]{:T(128)}, /*index=5*/s32[]{:T(128)}) while((s32[]{:T(128)}, f32[16,512]{1,0:T(8,128)S(1)}, s32[16,2]{0,1:T(2,128)S(1)}, f32[16,128]{1,0:T(8,128)S(1)}, s32[]{:T(128)}, /*index=5*/s32[]{:T(128)}) %tuple.69), condition=%wide.while_cond.1, body=%wide.while_body.1.sunk | while | flops 2 | bytes 2169 | solution.py:99
  75.1 1.4 dynamic-slice.17
  77.0 1.4 dynamic-slice.17
  79.0 1.4 dynamic-slice.17
  81.0 1.4 dynamic-slice.17
  83.0 1.4 dynamic-slice.17
  85.0 1.4 dynamic-slice.17
  87.0 1.4 dynamic-slice.17
  89.0 1.4 dynamic-slice.17
  91.0 1.4 dynamic-slice.17
  93.0 1.4 dynamic-slice.17
  95.0 1.4 dynamic-slice.17
  97.0 1.4 dynamic-slice.17
  99.0 1.4 dynamic-slice.17
  101.0 1.4 dynamic-slice.17
  103.0 1.4 dynamic-slice.17
  105.0 1.4 dynamic-slice.17
  113.5 2.1 fusion.186
  115.6 1.6 fusion.80
  117.2 1.6 fusion.78
  121.1 1.8 fusion.84
  122.9 35.6 %all-reduce.7 = f32[16]{0:T(128)S(1)} all-reduce(f32[16]{0:T(128)S(1)} %fusion.11), channel_id=3, replica_groups=mesh['grp'=2,'slab'=16] {'slab'}, use_global_device_ids=true, to_apply=%region_1.3.clone | all-reduce | flops 16 | bytes 128
  159.3 2.6 fusion.2
  171.1 39.7 %all-gather.1 = f32[32,68,64]{1,2,0:T(8,128)S(1)} all-gather(f32[1,68,64]{1,2,0:T(8,128)S(1)} %add_bitcast_fusion), channel_id=2, replica_groups=mesh['grp'=2,'slab'=16] {'grp','slab'}, dimensions={0}, use_global_device_ids=true | all-gather | bytes 574464 | tf_op jit(solution)/shard_map/all_gather | solution.py:121
  211.5 87.5 %reduce-scatter.2.cloned.1.call-done = f32[64,64]{1,0:T(8,128)} async-done(((f32[2048,64]{1,0:T(8,128)}), f32[64,64]{1,0:T(8,128)}) %reduce-scatter.2.cloned.1.call-update) | async-done | bytes 16400 | tf_op jit(solution)/shard_map/reduce_scatter | solution.py:120
  299.0 1.4 multiply_subtract_fusion.1
  300.3 39.3 %all_gather.9 = f32[2048,64]{1,0:T(8,128)S(1)} all-gather(f32[64,64]{1,0:T(8,128)S(1)} %get-tuple-element.61), channel_id=1, replica_groups=mesh['grp'=2,'slab'=16] {'grp','slab'}, dimensions={0}, use_global_device_ids=true | all-gather | bytes 540672 | tf_op jit(solution)/shard_map/all_gather | solution.py:127
  (203 shorter events, 59.6 us)
Async XLA Ops:
  7.2 9.2 %copy-start = (f32[8,8,512]{2,1,0:T(8,128)S(1)}, f32[8,8,512]{2,1,0:T(8,128)}, u32[]{:S(2)}) copy-start(f32[8,8,512]{2,1,0:T(8,128)} %param.11) | copy-start | bytes 393220
  7.2 10.2 %copy-start.5 = (f32[2048,64]{0,1:T(8,128)S(1)}, f32[2048,64]{0,1:T(8,128)}, u32[]{:S(2)}) copy-start(f32[2048,64]{0,1:T(8,128)} %param.17) | copy-start | bytes 1572868
  7.2 291.8 %reduce-scatter.2.cloned.1.call-start = ((), (), s32[]{:S(2)}) async-start(), calls=%async_computation.1 | async-start | bytes 1081344 | tf_op jit(solution)/shard_map/reduce_scatter | solution.py:120
  8.0 9.6 %collective-permute-start = (f32[1,8,512]{2,1,0:T(8,128)S(1)}, f32[1,8,512]{2,1,0:T(8,128)S(1)}, u32[]{:S(2)}, u32[]{:S(2)}) collective-permute-start(f32[1,8,512]{2,1,0:T(8,128)S(1)} %get-tuple-element.85), channel_id=1, source_target_pairs={{16,0},{17,1},{18,2},{19,3},{20,4},{21,5},{22,6},{23,7},{24,8},{25... | collective-permute-start | bytes 49160 | tf_op jit(solution)/shard_map/ppermute | solution.py:24
  9.3 8.3 %collective-permute-start.1 = (f32[1,8,512]{2,1,0:T(8,128)S(1)}, f32[1,8,512]{2,1,0:T(8,128)S(1)}, u32[]{:S(2)}, u32[]{:S(2)}) collective-permute-start(f32[1,8,512]{2,1,0:T(8,128)S(1)} %get-tuple-element.86), channel_id=1, source_target_pairs={{0,16},{1,17},{2,18},{3,19},{4,20},{5,21},{6,22},{7,23},{8,24},{9,... | collective-permute-start | bytes 49160 | tf_op jit(solution)/shard_map/ppermute | solution.py:22
  16.4 0.8 copy-start.2
  16.5 0.7 copy-start.11
  17.7 6.1 %collective-permute-start.2 = (f32[10,1,512]{2,1,0:T(1,128)S(1)}, f32[10,1,512]{2,1,0:T(1,128)S(1)}, u32[]{:S(2)}, u32[]{:S(2)}) collective-permute-start(f32[10,1,512]{2,1,0:T(1,128)S(1)} %get-tuple-element.73), channel_id=1, source_target_pairs={{1,0},{2,1},{3,2},{4,3},{5,4},{6,5},{7,6},{8,7},{9,8},{10,9},{11,1... | collective-permute-start | bytes 61448 | tf_op jit(solution)/shard_map/ppermute | solution.py:24
  19.0 4.8 %collective-permute-start.3 = (f32[10,1,512]{2,1,0:T(1,128)S(1)}, f32[10,1,512]{2,1,0:T(1,128)S(1)}, u32[]{:S(2)}, u32[]{:S(2)}) collective-permute-start(f32[10,1,512]{2,1,0:T(1,128)S(1)} %get-tuple-element.74), channel_id=1, source_target_pairs={{0,1},{1,2},{2,3},{3,4},{4,5},{5,6},{6,7},{7,8},{8,9},{9,10},{10,1... | collective-permute-start | bytes 61448 | tf_op jit(solution)/shard_map/ppermute | solution.py:22
  22.3 1.5 copy-start.8
  22.3 1.5 copy-start.9
  22.5 0.7 copy-start.13
  24.0 3.7 %collective-permute-start.5 = (f32[1,8,512]{2,1,0:T(8,128)S(1)}, f32[1,8,512]{2,1,0:T(8,128)S(1)}, u32[]{:S(2)}, u32[]{:S(2)}) collective-permute-start(f32[1,8,512]{2,1,0:T(8,128)S(1)} %get-tuple-element.75), channel_id=1, source_target_pairs={{0,16},{1,17},{2,18},{3,19},{4,20},{5,21},{6,22},{7,23},{8,24},{9,... | collective-permute-start | bytes 49160 | tf_op jit(solution)/shard_map/ppermute | solution.py:22
  26.2 5.6 %collective-permute-start.4 = (f32[1,8,512]{2,1,0:T(8,128)S(1)}, f32[1,8,512]{2,1,0:T(8,128)S(1)}, u32[]{:S(2)}, u32[]{:S(2)}) collective-permute-start(f32[1,8,512]{2,1,0:T(8,128)S(1)} %get-tuple-element.76), channel_id=1, source_target_pairs={{16,0},{17,1},{18,2},{19,3},{20,4},{21,5},{22,6},{23,7},{24,8},{25... | collective-permute-start | bytes 49160 | tf_op jit(solution)/shard_map/ppermute | solution.py:24
  31.9 5.3 %collective-permute-start.6 = (f32[10,1,512]{2,1,0:T(1,128)S(1)}, f32[10,1,512]{2,1,0:T(1,128)S(1)}, u32[]{:S(2)}, u32[]{:S(2)}) collective-permute-start(f32[10,1,512]{2,1,0:T(1,128)S(1)} %get-tuple-element.71), channel_id=1, source_target_pairs={{1,0},{2,1},{3,2},{4,3},{5,4},{6,5},{7,6},{8,7},{9,8},{10,9},{11,1... | collective-permute-start | bytes 61448 | tf_op jit(solution)/shard_map/ppermute | solution.py:24
  33.2 4.2 %collective-permute-start.7 = (f32[10,1,512]{2,1,0:T(1,128)S(1)}, f32[10,1,512]{2,1,0:T(1,128)S(1)}, u32[]{:S(2)}, u32[]{:S(2)}) collective-permute-start(f32[10,1,512]{2,1,0:T(1,128)S(1)} %get-tuple-element.72), channel_id=1, source_target_pairs={{0,1},{1,2},{2,3},{3,4},{4,5},{5,6},{6,7},{7,8},{8,9},{9,10},{10,1... | collective-permute-start | bytes 61448 | tf_op jit(solution)/shard_map/ppermute | solution.py:22
  120.2 0.7 copy-start.12
  159.3 2.6 copy-start.4
  161.9 1.0 copy-start.3
  161.9 1.0 copy-start.7
  162.9 1.0 copy-start.1
  166.1 1.0 copy-start.6
  210.9 88.1 %copy-start.10 = (f32[64,64]{1,0:T(8,128)S(1)}, f32[64,64]{1,0:T(8,128)}, u32[]{:S(2)}) copy-start(f32[64,64]{1,0:T(8,128)} %param.19) | copy-start | bytes 49156
Sparse Core Ops, SparseCore 0:
  166.2 132.7 reduce-scatter.1
